TPU v7x, 32 devices: a whole 2x2x4 slice. The times are simulated.
32 devices in a mesh: row: 8 (over y, x, core), col: 4 (over z).
Axes of the slice: x: 2, y: 2, z: 4, core: 2. Of those that a mesh axis runs over, the one named last changes fastest.
Arguments:
- matrix: float32 [8, 3, 256, 4, 6, 256], P('row', None, None, 'col'), as said below
- checksum: float32 [8, 3, 256, 6, 256], P('row'), as said below
- failed: int32 [4], P('col'), may hold values from 0 to 3, as said below
Outputs:
- factored: float32 [8, 3, 256, 4, 6, 256], P('row', None, None, 'col')
- updated_checksum_result: float32 [8, 3, 256, 6, 256], P('row')
Inputs may be any that keep to these rules, and one draw needn't show every extreme that they name: `failed`: a permutation of the grid column indices; entry 0 names the grid column whose tiles in matrix carry no information. With the lost grid column rebuilt from checksum, matrix is symmetric positive definite. `checksum`: for each grid row, the sum over all grid columns of the intact matrix's tiles, the lost column included.
All inputs are finite; a program needn't handle non-finite values.
Results may differ from a plain program's by a relative error of at most 0.0003.
Values sent between devices are 32-bit elements; how exact they have to be, the bound alone decides.
A program may use at most 128 MiB of HBM per device.

v0:
```python
import jax
import jax.numpy as jnp
from jax import lax
from jax.sharding import PartitionSpec as P

PANELS = 3
EXACT = lax.Precision.HIGHEST
FAST = lax.Precision.HIGH


def dot_t(a, b, precision=EXACT):
    return lax.dot_general(a, b, (((1,), (1,)), ((), ())), precision=precision)


def dot(a, b, precision=EXACT):
    return lax.dot_general(a, b, (((1,), (0,)), ((), ())), precision=precision)


def shards(matrix, checksum, failed):
    rows_count = lax.axis_size("row")
    cols_count = lax.axis_size("col")
    row_index = lax.axis_index("row")
    column_position = lax.axis_index("col")
    tile_rows, width, tile_cols = (matrix.shape[1], matrix.shape[2], matrix.shape[4])
    own = matrix.reshape(tile_rows, width, tile_cols, width).transpose(0, 2, 1, 3)
    totals = checksum.reshape(tile_rows, width, tile_cols, width).transpose(0, 2, 1, 3)
    row_tiles = row_index + jnp.arange(tile_rows, dtype=jnp.int32) * rows_count
    col_tiles = column_position + jnp.arange(tile_cols, dtype=jnp.int32) * cols_count
    slots = (PANELS - 1) // cols_count + 1
    top_slots = (PANELS - 1) // rows_count + 1
    lost_column = lax.all_gather(failed, "col", axis=0, tiled=True)[0]
    lost = column_position == lost_column
    gathered = lax.all_gather(own[:, :slots], "col", axis=0)
    ids = jnp.arange(cols_count, dtype=jnp.int32).reshape(-1, 1, 1, 1, 1)
    others = jnp.sum(jnp.where(ids != lost_column, gathered, 0.0), axis=0)
    patch = totals[:, :slots] - others
    panels = []
    for k in range(PANELS):
        slot = k // cols_count
        panels.append(
            jnp.where(
                lost_column == k % cols_count, patch[:, slot], gathered[k % cols_count, :, slot]
            )
        )
    lead = jnp.stack(
        [
            jnp.where(
                row_index == i % rows_count,
                jnp.stack(
                    [panels[k][i // rows_count] for k in range(i + 1)]
                    + [jnp.zeros((width, width), jnp.float32) for _ in range(i + 1, PANELS)]
                ),
                0.0,
            )
            for i in range(PANELS)
        ]
    )
    lead = lax.psum(lead, "row")
    need = [
        tile_cols if a < top_slots else min(tile_cols, (rows_count * (a + 1) - 1) // cols_count + 1)
        for a in range(tile_rows)
    ]
    packed = jnp.concatenate([own[a, : need[a]] for a in range(tile_rows)], axis=0)
    lead_done, packed = lax.optimization_barrier((lead, packed))
    lead = lead_done
    summed = lax.psum(jnp.where(lost, 0.0, packed), "col")
    filled = []
    start = 0
    for a in range(tile_rows):
        pad = jnp.zeros((tile_cols - need[a], width, width), jnp.float32)
        filled.append(jnp.concatenate([summed[start : start + need[a]], pad], axis=0))
        start += need[a]
    work = jnp.where(lost, totals - jnp.stack(filled), own)
    tops = jnp.stack(
        [
            jnp.where(
                row_index == i % rows_count,
                jnp.concatenate([work[i // rows_count], totals[i // rows_count]], axis=0),
                0.0,
            )
            for i in range(PANELS)
        ]
    )
    tops = lax.psum(tops, "row")
    identity = jnp.eye(width, dtype=jnp.float32)
    factor = {}
    inverse = []
    for k in range(PANELS):
        for i in range(k, PANELS):
            tile = lead[i, k]
            for m in range(k):
                tile = tile - dot_t(factor[i, m], factor[k, m])
            if i == k:
                factor[k, k] = jnp.linalg.cholesky(tile)
                inverse.append(
                    jax.scipy.linalg.solve_triangular(factor[k, k], identity, lower=True)
                )
            else:
                factor[i, k] = dot_t(tile, inverse[k])
    solved_rows = []
    for k in range(PANELS):
        block = panels[k].reshape(tile_rows * width, width)
        for m in range(k):
            block = block - dot_t(solved_rows[m], factor[k, m])
        block = dot_t(block, inverse[k]).reshape(tile_rows, width, width)
        block = jnp.where((row_tiles > k)[:, None, None], block, 0.0)
        block = jnp.where((row_tiles == k)[:, None, None], factor[k, k][None], block)
        solved_rows.append(block.reshape(tile_rows * width, width))
    flat = tops.transpose(0, 2, 1, 3).reshape(PANELS, width, 2 * tile_cols * width)
    solved_cols = []
    for k in range(PANELS):
        block = flat[k]
        for m in range(k):
            block = block - dot(factor[k, m], solved_cols[m])
        solved_cols.append(dot(inverse[k], block))
    rows_factor = jnp.concatenate(solved_rows, axis=1)
    cols_factor = jnp.concatenate(solved_cols, axis=0)
    split = tile_cols * width
    shape = (tile_rows, width, tile_cols, width)
    update = dot(rows_factor, cols_factor[:, :split], FAST).reshape(shape).transpose(0, 2, 1, 3)
    drop = dot(rows_factor, cols_factor[:, split:], FAST).reshape(shape).transpose(0, 2, 1, 3)
    new_totals = (totals - drop).transpose(0, 2, 1, 3)
    work = work - update
    front = []
    for b in range(slots):
        tiles = work[:, b]
        for k in range(PANELS):
            if k // cols_count == b:
                mine = solved_rows[k].reshape(tile_rows, width, width)
                tiles = jnp.where(column_position == k % cols_count, mine, tiles)
        front.append(tiles)
    work = jnp.concatenate([jnp.stack(front, axis=1), work[:, slots:]], axis=1)
    keep = (row_tiles[:, None] >= col_tiles[None, :])[:, :, None, None]
    factored = jnp.where(keep, work, 0.0).transpose(0, 2, 1, 3)
    return (factored.reshape(matrix.shape), new_totals.reshape(checksum.shape))


def solution(mesh):
    return jax.shard_map(
        shards,
        mesh=mesh,
        in_specs=(
            P("row", None, None, "col", None, None),
            P("row", None, None, None, None),
            P("col"),
        ),
        out_specs=(P("row", None, None, "col", None, None), P("row", None, None, None, None)),
        check_vma=False,
    )
```

profile of v0, /device:TPU:0, one launch (start us, length us, event | category | flops | bytes accessed | tf_op | source)
XLA Modules:
  0.0 600.1 jit_solution(15367717784824096456)
XLA Ops:
  7.2 12.1 %copy.79 = f32[1,3,256,1,6,256]{2,5,4,1,3,0:T(8,128)} copy(f32[1,3,256,1,6,256]{5,3,4,2,1,0:T(1,128)} %param.6) | data formatting | bytes 9437184 | tf_op args[0]
  23.7 9.9 %all-reduce.2 = s32[4]{0:T(128)S(1)} all-reduce(s32[4]{0:T(128)S(1)} %dynamic-update-slice.10), channel_id=1, replica_groups=mesh['row'=8,'col'=4] {'col'}, use_global_device_ids=true, to_apply=%add.2 | all-reduce | flops 4 | bytes 32
  44.4 43.6 %all-gather.3.cloned.1.call-done = f32[12,1,256,256]{3,2,1,0:T(8,128)} async-done(((f32[3,1,256,256]{3,2,1,0:T(8,128)}), f32[12,1,256,256]{3,2,1,0:T(8,128)}) %all-gather.3.cloned.1.call-update) | async-done | bytes 3145744 | tf_op jit(solution)/shard_map/all_gather | solution.py:33
  114.0 52.6 %all-reduce.7.cloned.1.call-done = f32[3,3,256,256]{2,3,1,0:T(8,128)} async-done(((f32[3,3,256,256]{2,3,1,0:T(8,128)}), f32[3,3,256,256]{2,3,1,0:T(8,128)}) %all-reduce.7.cloned.1.call-update) | async-done | bytes 2359312 | tf_op jit(solution)/shard_map/psum | solution.py:58
  173.6 11.7 %cholesky.172 = f32[128,128]{1,0:T(8,128)S(1)} custom-call(f32[128,128]{1,0:T(8,128)S(1)} %cholesky.270), custom_call_target="Cholesky" | custom-call | tf_op jit(solution)/shard_map/jit(cholesky)/cholesky | solution.py:94
  185.4 9.8 %custom-call.15 = f32[1,128,128]{1,2,0:T(8,128)S(1)} custom-call(f32[1,128,128]{2,1,0:T(8,128)S(1)} %get-tuple-element.105), custom_call_target="InvertDiagBlocksLowerTriangular" | custom-call | tf_op jit(solution)/shard_map/jit(cholesky)/cholesky | solution.py:94
  195.7 11.7 %cholesky.189 = f32[128,128]{1,0:T(8,128)S(1)} custom-call(f32[128,128]{1,0:T(8,128)S(1)} %convolution_subtract_fusion.15), custom_call_target="Cholesky" | custom-call | tf_op jit(solution)/shard_map/jit(cholesky)/cholesky | solution.py:94
  214.0 20.1 %custom-call.16 = f32[2,128,128]{1,2,0:T(8,128)S(1)} custom-call(f32[2,128,128]{2,1,0:T(8,128)S(1)} %get-tuple-element.28), custom_call_target="InvertDiagBlocksLowerTriangular" | custom-call | tf_op jit(solution)/shard_map/jit(_solve_triangular)/triangular_solve | solution.py:96
  238.1 11.7 %cholesky.206 = f32[128,128]{1,0:T(8,128)S(1)} custom-call(f32[128,128]{1,0:T(8,128)S(1)} %cholesky.273), custom_call_target="Cholesky" | custom-call | tf_op jit(solution)/shard_map/jit(cholesky)/cholesky | solution.py:94
  249.9 9.8 %custom-call.17 = f32[1,128,128]{1,2,0:T(8,128)S(1)} custom-call(f32[1,128,128]{2,1,0:T(8,128)S(1)} %get-tuple-element.101), custom_call_target="InvertDiagBlocksLowerTriangular" | custom-call | tf_op jit(solution)/shard_map/jit(cholesky)/cholesky | solution.py:94
  260.2 11.7 %cholesky.223 = f32[128,128]{1,0:T(8,128)S(1)} custom-call(f32[128,128]{1,0:T(8,128)S(1)} %convolution_subtract_fusion.14), custom_call_target="Cholesky" | custom-call | tf_op jit(solution)/shard_map/jit(cholesky)/cholesky | solution.py:94
  279.6 19.9 %custom-call.18 = f32[2,128,128]{1,2,0:T(8,128)S(1)} custom-call(f32[2,128,128]{2,1,0:T(8,128)S(1)} %get-tuple-element.29), custom_call_target="InvertDiagBlocksLowerTriangular" | custom-call | tf_op jit(solution)/shard_map/jit(_solve_triangular)/triangular_solve | solution.py:96
  304.8 20.6 %all-reduce.9.cloned.1.call-done = f32[16,256,256]{1,2,0:T(8,128)} async-done(((f32[16,256,256]{1,2,0:T(8,128)}), f32[16,256,256]{1,2,0:T(8,128)}) %all-reduce.9.cloned.1.call-update) | async-done | bytes 4194320 | tf_op jit(solution)/shard_map/psum | solution.py:66
  345.1 11.7 %cholesky.240 = f32[128,128]{1,0:T(8,128)S(1)} custom-call(f32[128,128]{1,0:T(8,128)S(1)} %cholesky.276), custom_call_target="Cholesky" | custom-call | tf_op jit(solution)/shard_map/jit(cholesky)/cholesky | solution.py:94
  356.9 10.2 %custom-call.19 = f32[1,128,128]{1,2,0:T(8,128)S(1)} custom-call(f32[1,128,128]{2,1,0:T(8,128)S(1)} %get-tuple-element.97), custom_call_target="InvertDiagBlocksLowerTriangular" | custom-call | tf_op jit(solution)/shard_map/jit(cholesky)/cholesky | solution.py:94
  367.5 11.7 %cholesky.257 = f32[128,128]{1,0:T(8,128)S(1)} custom-call(f32[128,128]{1,0:T(8,128)S(1)} %convolution_subtract_fusion.13), custom_call_target="Cholesky" | custom-call | tf_op jit(solution)/shard_map/jit(cholesky)/cholesky | solution.py:94
  386.6 20.3 %custom-call.20 = f32[2,128,128]{1,2,0:T(8,128)} custom-call(f32[2,128,128]{2,1,0:T(8,128)S(1)} %get-tuple-element.30), custom_call_target="InvertDiagBlocksLowerTriangular" | custom-call | tf_op jit(solution)/shard_map/jit(_solve_triangular)/triangular_solve | solution.py:96
  427.0 51.3 %all-reduce.11.cloned.1.call-done = f32[3,256,12,256]{1,3,2,0:T(8,128)} async-done(((f32[3,256,12,256]{1,3,2,0:T(8,128)}), f32[3,256,12,256]{1,3,2,0:T(8,128)}) %all-reduce.11.cloned.1.call-update) | async-done | bytes 9437200 | tf_op jit(solution)/shard_map/psum | solution.py:84
  478.3 7.5 %fusion.83 = (f32[1,256,12,256]{1,3,2,0:T(8,128)}, f32[1,256,12,256]{1,3,2,0:T(8,128)S(1)}, f32[1,256,12,256]{1,3,2,0:T(8,128)}) fusion(f32[3,256,12,256]{1,3,2,0:T(8,128)} %all-reduce.11.cloned.1.call-done), kind=kLoop, calls=%fused_computation.179 | loop fusion | bytes 18874368 | tf_op jit(solution)/shard_map/slice | solution.py:112
  515.6 7.7 %pad_maximum_fusion = f32[768,3072]{1,0:T(8,128)} fusion(f32[256,3072]{1,0:T(8,128)} %fusion.32, f32[256,3072]{1,0:T(8,128)} %copy-done, f32[256,3072]{1,0:T(8,128)S(1)} %fusion.37), kind=kLoop, calls=%fused_computation.7 | loop fusion | flops 4718592 | bytes 18874368 | tf_op jit(solution)/shard_map/concatenate | solution.py:117
  523.3 10.0 %fusion.2 = f32[768,1536]{1,0:T(8,128)} fusion(f32[768,3072]{1,0:T(8,128)} %pad_maximum_fusion, f32[768,256]{1,0:T(8,128)} %get-tuple-element.114, f32[768,256]{1,0:T(8,128)} %get-tuple-element.112, f32[768,256]{1,0:T(8,128)} %bitcast.226), kind=kOutput, calls=%fused_computation.11 | convolution fusion | flops 5436997632 | bytes 11796480 | tf_op jit(solution)/shard_map/dot_general | solution.py:16
  533.3 7.7 %fusion = f32[768,1536]{1,0:T(8,128)} fusion(f32[768,3072]{1,0:T(8,128)S(1)} %copy-done.5, f32[768,256]{1,0:T(8,128)S(1)} %copy-done.39, f32[768,256]{1,0:T(8,128)S(1)} %copy-done.24, f32[768,256]{1,0:T(8,128)S(1)} %bitcast.227), kind=kOutput, calls=%fused_computation.9 | convolution fusion | flops 5436997632 | bytes 11796480 | tf_op jit(solution)/shard_map/dot_general | solution.py:16
  563.3 12.1 %copy.109 = f32[1,3,256,1,6,256]{5,3,4,2,1,0:T(1,128)} copy(f32[1,3,256,1,6,256]{2,5,4,1,3,0:T(8,128)} %fusion.5) | data formatting | bytes 9437184
  582.5 7.2 %copy_subtract_fusion = f32[1,3,256,6,256]{4,3,2,1,0:T(8,128)S(1)} fusion(f32[1,3,256,6,256]{4,3,2,1,0:T(8,128)} %reshape.319, f32[1,3,256,6,256]{4,2,3,1,0:T(8,128)} %param.7), kind=kLoop, calls=%fused_computation.8 | loop fusion | flops 1179648 | bytes 14155776 | tf_op jit(solution)/shard_map/sub | solution.py:122
  (275 shorter events, 189.7 us)
Async XLA Ops:
  7.2 80.9 %all-gather.3.cloned.1.call-start = ((), (), s32[]{:S(2)}) async-start(), calls=%async_computation.3 | async-start | bytes 3932160 | tf_op jit(solution)/shard_map/all_gather | solution.py:33
  21.7 145.0 %all-reduce.7.cloned.1.call-start = ((), (), s32[]{:S(2)}) async-start(), calls=%async_computation | async-start | bytes 4718592 | tf_op jit(solution)/shard_map/psum | solution.py:58
  104.9 220.5 %all-reduce.9.cloned.1.call-start = ((), (), s32[]{:S(2)}) async-start(), calls=%async_computation.1 | async-start | bytes 8388608 | tf_op jit(solution)/shard_map/psum | solution.py:66
  105.0 194.8 %copy-start.13 = (f32[256,256]{1,0:T(8,128)}, f32[256,256]{1,0:T(8,128)S(1)}, u32[]{:S(2)}) copy-start(f32[256,256]{1,0:T(8,128)S(1)} %fusion.31) | copy-start | bytes 786436
  171.3 307.1 %all-reduce.11.cloned.1.call-start = ((), (), s32[]{:S(2)}) async-start(), calls=%async_computation.2 | async-start | bytes 18874368 | tf_op jit(solution)/shard_map/psum | solution.py:84
  235.0 172.1 %copy-start.18 = (f32[128,256]{1,0:T(8,128)}, f32[128,256]{1,0:T(8,128)S(1)}, u32[]{:S(2)}) copy-start(f32[128,256]{1,0:T(8,128)S(1)} %fusion.53) | copy-start | bytes 393220
  279.6 45.7 %copy-start.52 = (s32[2,2]{1,0:T(2,128)}, s32[2,2]{1,0:T(2,128)S(1)}, u32[]{:S(2)}) copy-start(s32[2,2]{1,0:T(2,128)S(1)} %get-tuple-element.277) | copy-start | bytes 52
  299.8 41.5 %copy-start.15 = (f32[128,256]{1,0:T(8,128)}, f32[128,256]{1,0:T(8,128)S(1)}, u32[]{:S(2)}) copy-start(f32[128,256]{1,0:T(8,128)S(1)} %fusion.40) | copy-start | bytes 393220
  302.6 119.8 %copy-start.4 = (f32[256,256]{1,0:T(8,128)}, f32[256,256]{1,0:T(8,128)S(1)}, u32[]{:S(2)}) copy-start(f32[256,256]{1,0:T(8,128)S(1)} %fusion.22) | copy-start | bytes 786436
  342.4 40.3 %copy-start.53 = (s32[2,2]{1,0:T(2,128)S(1)}, s32[2,2]{1,0:T(2,128)}, u32[]{:S(2)}) copy-start(s32[2,2]{1,0:T(2,128)} %copy-done.52) | copy-start | bytes 52
  343.0 80.3 %copy-start.10 = (f32[256,256]{1,0:T(8,128)}, f32[256,256]{1,0:T(8,128)S(1)}, u32[]{:S(2)}) copy-start(f32[256,256]{1,0:T(8,128)S(1)} %fusion.36) | copy-start | bytes 786436
  343.0 64.0 %copy-start.38 = (f32[256,256]{1,0:T(8,128)S(1)}, f32[256,256]{1,0:T(8,128)}, u32[]{:S(2)}) copy-start(f32[256,256]{1,0:T(8,128)} %get-tuple-element.68) | copy-start | bytes 786436
  344.5 62.6 %copy-start.50 = (pred[3]{0:T(512)(128)(4,1)S(1)}, pred[3]{0:T(512)(128)(4,1)}, u32[]{:S(2)}) copy-start(pred[3]{0:T(512)(128)(4,1)} %get-tuple-element.116) | copy-start | bytes 13
  344.5 62.6 %copy-start.51 = (pred[3]{0:T(512)(128)(4,1)S(1)}, pred[3]{0:T(512)(128)(4,1)}, u32[]{:S(2)}) copy-start(pred[3]{0:T(512)(128)(4,1)} %get-tuple-element.117) | copy-start | bytes 13
  386.6 20.4 %copy-start.32 = (f32[256,256]{1,0:T(8,128)}, f32[256,256]{1,0:T(8,128)S(1)}, u32[]{:S(2)}) copy-start(f32[256,256]{1,0:T(8,128)S(1)} %get-tuple-element.272) | copy-start | bytes 786436
  408.0 6.6 %copy-start.6 = (f32[3,256,256]{1,2,0:T(8,128)}, f32[3,256,256]{1,2,0:T(8,128)S(1)}, u32[]{:S(2)}) copy-start(f32[3,256,256]{1,2,0:T(8,128)S(1)} %fusion.9) | copy-start | bytes 2359300
  408.3 14.1 %copy-start.8 = (f32[3,256,256]{2,1,0:T(8,128)}, f32[3,256,256]{2,1,0:T(8,128)S(1)}, u32[]{:S(2)}) copy-start(f32[3,256,256]{2,1,0:T(8,128)S(1)} %copy.97) | copy-start | bytes 2359300
  412.6 6.3 %copy-start.14 = (f32[256,256]{1,0:T(8,128)S(1)}, f32[256,256]{1,0:T(8,128)}, u32[]{:S(2)}) copy-start(f32[256,256]{1,0:T(8,128)} %copy-done.13) | copy-start | bytes 786436
  414.6 7.8 %copy-start.22 = (f32[3,1,256,256]{3,2,0,1:T(8,128)S(1)}, f32[3,1,256,256]{3,2,0,1:T(8,128)}, u32[]{:S(2)}) copy-start(f32[3,1,256,256]{3,2,0,1:T(8,128)} %copy.93) | copy-start | bytes 2359300
  414.6 8.7 %copy-start.23 = (f32[768,256]{1,0:T(8,128)S(1)}, f32[768,256]{1,0:T(8,128)}, u32[]{:S(2)}) copy-start(f32[768,256]{1,0:T(8,128)} %get-tuple-element.112) | copy-start | bytes 2359300
  523.3 10.0 %copy-start.5 = (f32[768,3072]{1,0:T(8,128)S(1)}, f32[768,3072]{1,0:T(8,128)}, u32[]{:S(2)}) copy-start(f32[768,3072]{1,0:T(8,128)} %pad_maximum_fusion) | copy-start | bytes 28311556
  523.3 10.0 %copy-start.9 = (f32[3,256,256]{2,1,0:T(8,128)S(1)}, f32[3,256,256]{2,1,0:T(8,128)}, u32[]{:S(2)}) copy-start(f32[3,256,256]{2,1,0:T(8,128)} %copy-done.8) | copy-start | bytes 2359300
  523.3 10.0 %copy-start.24 = (f32[768,256]{1,0:T(8,128)S(1)}, f32[768,256]{1,0:T(8,128)}, u32[]{:S(2)}) copy-start(f32[768,256]{1,0:T(8,128)} %get-tuple-element.112) | copy-start | bytes 2359300
  523.3 10.0 %copy-start.39 = (f32[768,256]{1,0:T(8,128)S(1)}, f32[768,256]{1,0:T(8,128)}, u32[]{:S(2)}) copy-start(f32[768,256]{1,0:T(8,128)} %get-tuple-element.114) | copy-start | bytes 2359300
  (37 other events, 100.9 us)
Sparse Core Ops, SparseCore 0:
  21.8 66.1 all-gather.2
  105.0 61.5 all-reduce.6
  171.4 153.9 all-reduce.8
  341.5 136.7 all-reduce.10
where the time goes:
time: 606 us; the launch traced here: 600 us
  other arithmetic  213 us (35%)
  waiting for transfers between devices  168 us (28%)
  local copies, waits for them, and re-layouts  122 us (20%)
  matrix products  65.9 us (11%)
  between operations  19.8 us (3%)
  blocking collectives  9.92 us (2%)
    another operation x20, other arithmetic, shards(): factor[k, k] = jnp.linalg.cholesky(tile)  104 us
    another operation x7, other arithmetic, shards(): jax.scipy.linalg.solve_triangular(factor[k, k], identity, lower=True)  62.5 us
    psum x1, waiting for transfers between devices, shards(): lead = lax.psum(lead, 'row')  52.6 us
    psum x1, waiting for transfers between devices, shards(): tops = lax.psum(tops, 'row')  51.3 us
    unnamed x124, local copies, waits for them, and re-layouts  46.6 us
    all_gather x1, waiting for transfers between devices, shards(): gathered = lax.all_gather(own[:, :slots], 'col', axis=0)  43.6 us
    dot_general x8, matrix products, dot(): return lax.dot_general(a, b, (((1,), (0,)), ((), ())), precision=precision)  41.3 us
    psum x1, waiting for transfers between devices, shards(): summed = lax.psum(jnp.where(lost, 0.0, packed), 'col')  20.6 us
  transfers between devices with their start and end apart: 4, of which 4 were waited for; matrix products, arithmetic and copies ran while one was open for 39% of the time, Pallas kernels for 0%

commit v1 on v0

--- a/solution.py
+++ b/solution.py
@@ -55,7 +55,7 @@
             for i in range(PANELS)
         ]
     )
-    lead = lax.psum(lead, "row")
+    lead = jnp.sum(lax.all_gather(lead, "row"), axis=0)
     need = [
         tile_cols if a < top_slots else min(tile_cols, (rows_count * (a + 1) - 1) // cols_count + 1)
         for a in range(tile_rows)

time: 606 us -> 636 us (1.050)
  waiting for transfers between devices: 168 us -> 197 us
  other arithmetic: 213 us -> 228 us
  local copies, waits for them, and re-layouts: 122 us -> 110 us
    all_gather x0 -> x1, waiting for transfers between devices: none -> 85.4 us  [shards(): lead = jnp.sum(lax.all_gather(lead, 'row'), axis=0)]
    psum x1 -> x0, waiting for transfers between devices: 52.6 us -> none  [shards(): lead = lax.psum(lead, 'row')]
    unnamed x124 -> x133, local copies, waits for them, and re-layouts: 46.6 us -> 35.2 us
    psum x1, waiting for transfers between devices: 20.6 us -> 10.1 us  [shards(): summed = lax.psum(jnp.where(lost, 0.0, packed), 'col')]
    slice x1 -> x4, local copies, waits for them, and re-layouts: 7.46 us -> 16.9 us  [shards(): block = flat[k]]
    reduce_sum x0 -> x1, other arithmetic: none -> 7.94 us  [shards(): lead = jnp.sum(lax.all_gather(lead, 'row'), axis=0)]
    select_n x6 -> x0, local copies, waits for them, and re-layouts: 6.88 us -> none  [the longest x3 4.25 us: shards(): factor[k, k] = jnp.linalg.cholesky(tile)]
    another operation x22, local copies, waits for them, and re-layouts: 12 us -> 18.4 us  [shards(): jax.scipy.linalg.solve_triangular(factor[k, k], identity, lower=True)]
  transfers between devices with their start and end apart: 4 -> 4, of which waited for: 4 -> 4; matrix products, arithmetic and copies ran while one was open for 39% -> 38% of each run, Pallas kernels for 0% -> 0%
where the time goes in v1:
time: 636 us; the launch traced here: 629 us
  other arithmetic  228 us (36%)
  waiting for transfers between devices  197 us (31%)
  local copies, waits for them, and re-layouts  110 us (17%)
  matrix products  63.3 us (10%)
  between operations  19.7 us (3%)
  blocking collectives  9.92 us (2%)
    another operation x20, other arithmetic, shards(): factor[k, k] = jnp.linalg.cholesky(tile)  105 us
    all_gather x1, waiting for transfers between devices, shards(): lead = jnp.sum(lax.all_gather(lead, 'row'), axis=0)  85.4 us
    another operation x7, other arithmetic, shards(): jax.scipy.linalg.solve_triangular(factor[k, k], identity, lower=True)  66.2 us
    psum x1, waiting for transfers between devices, shards(): tops = lax.psum(tops, 'row')  52.5 us
    all_gather x1, waiting for transfers between devices, shards(): gathered = lax.all_gather(own[:, :slots], 'col', axis=0)  49.1 us
    dot_general x8, matrix products, dot(): return lax.dot_general(a, b, (((1,), (0,)), ((), ())), precision=precision)  39.7 us
    unnamed x133, local copies, waits for them, and re-layouts  35.2 us
    another operation x22, local copies, waits for them, and re-layouts, shards(): jax.scipy.linalg.solve_triangular(factor[k, k], identity, lower=True)  18.4 us
  transfers between devices with their start and end apart: 4, of which 4 were waited for; matrix products, arithmetic and copies ran while one was open for 38% of the time, Pallas kernels for 0%

profile of v1, /device:TPU:0, one launch (start us, length us, event | category | flops | bytes accessed | tf_op | source)
XLA Modules:
  0.0 629.4 jit_solution(950692530796132830)
XLA Ops:
  15.4 9.9 %all-reduce.2 = s32[4]{0:T(128)S(1)} all-reduce(s32[4]{0:T(128)S(1)} %dynamic-update-slice.10), channel_id=1, replica_groups=mesh['row'=8,'col'=4] {'col'}, use_global_device_ids=true, to_apply=%add.2 | all-reduce | flops 4 | bytes 32
  30.5 49.1 %all-gather.5.cloned.1.call-done = f32[12,1,256,256]{3,2,1,0:T(8,128)} async-done(((f32[3,1,256,256]{3,2,1,0:T(8,128)}), f32[12,1,256,256]{3,2,1,0:T(8,128)}) %all-gather.5.cloned.1.call-update) | async-done | bytes 3145744 | tf_op jit(solution)/shard_map/all_gather | solution.py:33
  100.6 85.4 %all-gather.7.cloned.1.call-done = f32[24,3,256,256]{3,2,1,0:T(8,128)} async-done(((f32[3,3,256,256]{3,2,1,0:T(8,128)}), f32[24,3,256,256]{3,2,1,0:T(8,128)}) %all-gather.7.cloned.1.call-update) | async-done | bytes 18874384 | tf_op jit(solution)/shard_map/all_gather | solution.py:58
  186.0 7.9 %reduce_sum.22 = f32[3,3,256,256]{3,2,1,0:T(8,128)S(1)} reduce(f32[8,3,3,256,256]{4,3,2,1,0:T(8,128)} %bitcast.233, f32[]{:T(128)} %constant.84.clone.1), dimensions={0}, to_apply=%region_1.2 | reduce | flops 4128768 | bytes 21233668 | tf_op jit(solution)/shard_map/reduce_sum | solution.py:58
  202.9 11.7 %cholesky.172 = f32[128,128]{1,0:T(8,128)S(1)} custom-call(f32[128,128]{1,0:T(8,128)S(1)} %cholesky.270), custom_call_target="Cholesky" | custom-call | tf_op jit(solution)/shard_map/jit(cholesky)/cholesky | solution.py:94
  214.7 9.8 %custom-call.15 = f32[1,128,128]{1,2,0:T(8,128)S(1)} custom-call(f32[1,128,128]{2,1,0:T(8,128)S(1)} %get-tuple-element.100), custom_call_target="InvertDiagBlocksLowerTriangular" | custom-call | tf_op jit(solution)/shard_map/jit(cholesky)/cholesky | solution.py:94
  225.0 11.7 %cholesky.189 = f32[128,128]{1,0:T(8,128)S(1)} custom-call(f32[128,128]{1,0:T(8,128)S(1)} %convolution_subtract_fusion.15), custom_call_target="Cholesky" | custom-call | tf_op jit(solution)/shard_map/jit(cholesky)/cholesky | solution.py:94
  244.2 20.2 %custom-call.16 = f32[2,128,128]{1,2,0:T(8,128)S(1)} custom-call(f32[2,128,128]{2,1,0:T(8,128)S(1)} %get-tuple-element.28), custom_call_target="InvertDiagBlocksLowerTriangular" | custom-call | tf_op jit(solution)/shard_map/jit(_solve_triangular)/triangular_solve | solution.py:96
  269.7 11.7 %cholesky.206 = f32[128,128]{1,0:T(8,128)S(1)} custom-call(f32[128,128]{1,0:T(8,128)S(1)} %cholesky.273), custom_call_target="Cholesky" | custom-call | tf_op jit(solution)/shard_map/jit(cholesky)/cholesky | solution.py:94
  282.0 10.4 %custom-call.17 = f32[1,128,128]{1,2,0:T(8,128)} custom-call(f32[1,128,128]{2,1,0:T(8,128)S(1)} %get-tuple-element.96), custom_call_target="InvertDiagBlocksLowerTriangular" | custom-call | tf_op jit(solution)/shard_map/jit(cholesky)/cholesky | solution.py:94
  294.6 11.7 %cholesky.223 = f32[128,128]{1,0:T(8,128)S(1)} custom-call(f32[128,128]{1,0:T(8,128)S(1)} %convolution_subtract_fusion.14), custom_call_target="Cholesky" | custom-call | tf_op jit(solution)/shard_map/jit(cholesky)/cholesky | solution.py:94
  318.1 20.6 %custom-call.18 = f32[2,128,128]{1,2,0:T(8,128)S(1)} custom-call(f32[2,128,128]{2,1,0:T(8,128)} %copy-done.48), custom_call_target="InvertDiagBlocksLowerTriangular" | custom-call | tf_op jit(solution)/shard_map/jit(_solve_triangular)/triangular_solve | solution.py:96
  342.8 10.1 %all-reduce.6.cloned.1.call-done = f32[16,256,256]{2,1,0:T(8,128)} async-done(((f32[16,256,256]{2,1,0:T(8,128)}), f32[16,256,256]{2,1,0:T(8,128)}) %all-reduce.6.cloned.1.call-update) | async-done | bytes 4194320 | tf_op jit(solution)/shard_map/psum | solution.py:66
  373.6 11.7 %cholesky.240 = f32[128,128]{1,0:T(8,128)S(1)} custom-call(f32[128,128]{1,0:T(8,128)S(1)} %cholesky.276), custom_call_target="Cholesky" | custom-call | tf_op jit(solution)/shard_map/jit(cholesky)/cholesky | solution.py:94
  385.4 9.8 %custom-call.19 = f32[1,128,128]{1,2,0:T(8,128)S(1)} custom-call(f32[1,128,128]{2,1,0:T(8,128)S(1)} %get-tuple-element.92), custom_call_target="InvertDiagBlocksLowerTriangular" | custom-call | tf_op jit(solution)/shard_map/jit(cholesky)/cholesky | solution.py:94
  397.4 12.1 %cholesky.257 = f32[128,128]{1,0:T(8,128)S(1)} custom-call(f32[128,128]{1,0:T(8,128)S(1)} %convolution_subtract_fusion.13), custom_call_target="Cholesky" | custom-call | tf_op jit(solution)/shard_map/jit(cholesky)/cholesky | solution.py:94
  414.6 8.3 %while.8 = (s32[]{:T(128)}, f32[256,256]{1,0:T(8,128)}, s32[2,2]{1,0:T(2,128)}, f32[2,128,128]{2,1,0:T(8,128)}, s32[]{:T(128)}) while((s32[]{:T(128)}, f32[256,256]{1,0:T(8,128)}, s32[2,2]{1,0:T(2,128)}, f32[2,128,128]{2,1,0:T(8,128)}, s32[]{:T(128)}) %tuple.105), condition=%wide.while_cond.clone.1, body=%wide.while_body.clone.1.sunk | while | flops 2 | bytes 132205 | solution.py:96
  422.9 21.1 %custom-call.20 = f32[2,128,128]{1,2,0:T(8,128)} custom-call(f32[2,128,128]{2,1,0:T(8,128)} %get-tuple-element.30), custom_call_target="InvertDiagBlocksLowerTriangular" | custom-call | tf_op jit(solution)/shard_map/jit(_solve_triangular)/triangular_solve | solution.py:96
  454.0 52.5 %all-reduce.8.cloned.1.call-done = f32[3,256,12,256]{3,1,0,2:T(8,128)} async-done(((f32[3,256,12,256]{3,1,0,2:T(8,128)}), f32[3,256,12,256]{3,1,0,2:T(8,128)}) %all-reduce.8.cloned.1.call-update) | async-done | bytes 9437200 | tf_op jit(solution)/shard_map/psum | solution.py:84
  506.5 7.4 %fusion.83 = (f32[1,256,12,256]{3,1,0,2:T(8,128)}, f32[1,256,12,256]{3,1,0,2:T(8,128)}, f32[1,256,12,256]{3,1,0,2:T(8,128)S(1)}) fusion(f32[3,256,12,256]{3,1,0,2:T(8,128)} %all-reduce.8.cloned.1.call-done), kind=kLoop, calls=%fused_computation.183 | loop fusion | bytes 18874368 | tf_op jit(solution)/shard_map/slice | solution.py:112
  552.3 7.6 %pad_maximum_fusion = f32[768,3072]{1,0:T(8,128)} fusion(f32[256,3072]{1,0:T(8,128)} %fusion.32, f32[256,3072]{1,0:T(8,128)} %copy-done, f32[256,3072]{1,0:T(8,128)S(1)} %fusion.37), kind=kLoop, calls=%fused_computation.7 | loop fusion | flops 4718592 | bytes 18874368 | tf_op jit(solution)/shard_map/concatenate | solution.py:117
  559.9 10.1 %fusion = f32[768,1536]{1,0:T(8,128)} fusion(f32[768,3072]{1,0:T(8,128)} %pad_maximum_fusion, f32[768,256]{1,0:T(8,128)} %get-tuple-element.109, f32[768,256]{1,0:T(8,128)} %copy-done.27, f32[768,256]{1,0:T(8,128)} %bitcast.242), kind=kOutput, calls=%fused_computation.9 | convolution fusion | flops 5436997632 | bytes 11796480 | tf_op jit(solution)/shard_map/dot_general | solution.py:16
  570.1 8.0 %fusion.2 = f32[768,1536]{1,0:T(8,128)} fusion(f32[768,3072]{1,0:T(8,128)S(1)} %copy-done.10, f32[768,256]{1,0:T(8,128)S(1)} %copy-done.46, f32[768,256]{1,0:T(8,128)S(1)} %copy-done.28, f32[768,256]{1,0:T(8,128)S(1)} %bitcast.243), kind=kOutput, calls=%fused_computation.11 | convolution fusion | flops 5436997632 | bytes 11796480 | tf_op jit(solution)/shard_map/dot_general | solution.py:16
  595.5 9.4 %copy.73 = f32[1,3,256,1,6,256]{5,3,4,2,1,0:T(1,128)} copy(f32[1,3,256,1,6,256]{5,2,1,4,3,0:T(8,128)} %fusion.5) | data formatting | bytes 9437184
  (278 shorter events, 198.9 us)
Async XLA Ops:
  7.2 6.9 %copy-start.60 = (u32[32]{0:T(128)S(1)}, u32[32]{0:T(128)}, u32[]{:S(2)}) copy-start(u32[32]{0:T(128)} %constant.117) | copy-start | bytes 388
  7.2 72.5 %all-gather.5.cloned.1.call-start = ((), (), s32[]{:S(2)}) async-start(), calls=%async_computation.2 | async-start | bytes 3932160 | tf_op jit(solution)/shard_map/all_gather | solution.py:33
  13.4 172.6 %all-gather.7.cloned.1.call-start = ((), (), s32[]{:S(2)}) async-start(), calls=%async_computation.3 | async-start | bytes 21233664 | tf_op jit(solution)/shard_map/all_gather | solution.py:58
  88.6 264.3 %all-reduce.6.cloned.1.call-start = ((), (), s32[]{:S(2)}) async-start(), calls=%async_computation | async-start | bytes 8388608 | tf_op jit(solution)/shard_map/psum | solution.py:66
  91.5 6.0 copy-start.52
  92.2 5.2 copy-start.54
  92.2 5.2 copy-start.56
  198.5 307.9 %all-reduce.8.cloned.1.call-start = ((), (), s32[]{:S(2)}) async-start(), calls=%async_computation.1 | async-start | bytes 18874368 | tf_op jit(solution)/shard_map/psum | solution.py:84
  265.4 75.8 %copy-start.23 = (f32[128,256]{1,0:T(8,128)}, f32[128,256]{1,0:T(8,128)S(1)}, u32[]{:S(2)}) copy-start(f32[128,256]{1,0:T(8,128)S(1)} %fusion.53) | copy-start | bytes 393220
  341.6 108.6 %copy-start.8 = (f32[256,256]{1,0:T(8,128)}, f32[256,256]{1,0:T(8,128)S(1)}, u32[]{:S(2)}) copy-start(f32[256,256]{1,0:T(8,128)S(1)} %fusion.22) | copy-start | bytes 786436
  370.8 80.3 %copy-start.11 = (f32[256,256]{1,0:T(8,128)}, f32[256,256]{1,0:T(8,128)S(1)}, u32[]{:S(2)}) copy-start(f32[256,256]{1,0:T(8,128)S(1)} %fusion.36) | copy-start | bytes 786436
  370.8 73.2 %copy-start.19 = (f32[3,1,256,256]{3,2,0,1:T(8,128)S(1)}, f32[3,1,256,256]{3,2,0,1:T(8,128)}, u32[]{:S(2)}) copy-start(f32[3,1,256,256]{3,2,0,1:T(8,128)} %copy-done.18) | copy-start | bytes 2359300
  370.8 73.2 %copy-start.24 = (f32[128,256]{1,0:T(8,128)S(1)}, f32[128,256]{1,0:T(8,128)}, u32[]{:S(2)}) copy-start(f32[128,256]{1,0:T(8,128)} %copy-done.23) | copy-start | bytes 393220
  372.7 73.1 %copy-start.17 = (f32[3,1,256,256]{3,2,0,1:T(8,128)S(1)}, f32[3,1,256,256]{3,2,0,1:T(8,128)}, u32[]{:S(2)}) copy-start(f32[3,1,256,256]{3,2,0,1:T(8,128)} %copy-done.16) | copy-start | bytes 2359300
  412.1 34.6 %copy-start.29 = (f32[256,256]{1,0:T(8,128)S(1)}, f32[256,256]{1,0:T(8,128)}, u32[]{:S(2)}) copy-start(f32[256,256]{1,0:T(8,128)} %get-tuple-element.64) | copy-start | bytes 786436
  413.8 38.1 %copy-start.31 = (f32[256,256]{1,0:T(8,128)}, f32[256,256]{1,0:T(8,128)S(1)}, u32[]{:S(2)}) copy-start(f32[256,256]{1,0:T(8,128)S(1)} %get-tuple-element.62) | copy-start | bytes 786436
  445.8 4.4 copy-start.5
  445.8 4.4 copy-start.15
  530.5 4.9 copy-start.4
  530.5 4.9 copy-start.9
  559.9 10.1 %copy-start.6 = (f32[3,256,256]{2,1,0:T(8,128)S(1)}, f32[3,256,256]{2,1,0:T(8,128)}, u32[]{:S(2)}) copy-start(f32[3,256,256]{2,1,0:T(8,128)} %copy-done.5) | copy-start | bytes 2359300
  559.9 10.1 %copy-start.10 = (f32[768,3072]{1,0:T(8,128)S(1)}, f32[768,3072]{1,0:T(8,128)}, u32[]{:S(2)}) copy-start(f32[768,3072]{1,0:T(8,128)} %pad_maximum_fusion) | copy-start | bytes 28311556
  559.9 10.1 %copy-start.28 = (f32[768,256]{1,0:T(8,128)S(1)}, f32[768,256]{1,0:T(8,128)}, u32[]{:S(2)}) copy-start(f32[768,256]{1,0:T(8,128)} %copy-done.27) | copy-start | bytes 2359300
  559.9 10.1 %copy-start.46 = (f32[768,256]{1,0:T(8,128)S(1)}, f32[768,256]{1,0:T(8,128)}, u32[]{:S(2)}) copy-start(f32[768,256]{1,0:T(8,128)} %get-tuple-element.109) | copy-start | bytes 2359300
  (43 other events, 84.8 us)
Sparse Core Ops, SparseCore 0:
  13.5 66.1 all-gather.4
  88.7 97.2 all-gather.6
  198.7 154.1 all-reduce.5
  369.4 136.9 all-reduce.7
